TPU v7x, 32 devices: a whole 2x2x4 slice. The times are simulated.
32 devices in a mesh: groups: 2 (over y), chan: 4 (over z), tm: 2 (over core), dp: 2 (over x).
Axes of the slice: x: 2, y: 2, z: 4, core: 2. Of those that a mesh axis runs over, the one named last changes fastest.
Arguments:
- features: bfloat16 [384, 4, 8, 256], P('chan', ('groups', 'dp'), 'tm'), parts along dimension 1, may hold values from -6 to 6
- kernel: bfloat16 [384, 27, 384], P('chan'), may hold values from -0.078125 to 0.078125
- cotangent: bfloat16 [384, 4, 8, 256], P('chan', ('groups', 'dp'), 'tm'), parts along dimension 1, may hold values from -6 to 6
Outputs:
- conv_out: bfloat16 [384, 4, 8, 256], P('chan', ('groups', 'dp'), 'tm'), parts along dimension 1
- feature_grad: bfloat16 [384, 4, 8, 256], P('chan', ('groups', 'dp'), 'tm'), parts along dimension 1
- kernel_grad: float32 [768, 27, 384], P(('groups', 'chan')), parts along dimension 0
There are 2 independent parts, one for each index of `groups`. A program takes and returns all parts, laid end to end along the dimension named above; an argument that names none is the same for every part. Nothing has to cross between parts.
All inputs are finite; a program needn't handle non-finite values.
Results may differ from a plain program's by a relative error of at most 0.0051.
Values may be sent and summed in bfloat16 or wider, within the bound.
A program may use at most 128 MiB of HBM per device.

v0:
```python
import math

import jax
import jax.numpy as jnp
from jax import lax
from jax.sharding import PartitionSpec as P

WID = 64


def from_behind(x, axis, by):
    size = lax.axis_size(axis)
    pairs = [(i, i + by) for i in range(size) if 0 <= i + by < size]
    return lax.ppermute(x, axis, pairs)


def padded_copies(block):
    pixels = block.shape[-1]
    column = lax.broadcasted_iota(jnp.int32, (pixels,), 0) % WID
    nothing = jnp.zeros((), block.dtype)
    widths = [(0, 0), (0, 0), (0, 0), (WID + 1, WID + 1)]
    left_cut = jnp.pad(jnp.where(column == WID - 1, nothing, block), widths)
    untouched = jnp.pad(block, widths)
    right_cut = jnp.pad(jnp.where(column == 0, nothing, block), widths)
    return (left_cut, untouched, right_cut)


def tap_window(copies, first_frame, vertical, horizontal, frames, pixels):
    source = copies[horizontal]
    offset = vertical * WID + horizontal
    return source[:, :, first_frame : first_frame + frames, offset : offset + pixels]


def stacked_taps(copies, first_frame, flipped, frames, pixels):
    pieces = []
    for vertical in range(3):
        for horizontal in range(3):
            if flipped:
                pieces.append(
                    tap_window(copies, first_frame, 2 - vertical, 2 - horizontal, frames, pixels)
                )
            else:
                pieces.append(tap_window(copies, first_frame, vertical, horizontal, frames, pixels))
    concatenated = jnp.concatenate(pieces, axis=0)
    return concatenated.reshape(concatenated.shape[0], -1)


def local(features, kernel, cotangent):
    channels, clip_count, frames, pixels = features.shape
    flat_length = clip_count * frames * pixels
    widened = features.astype(jnp.float32)
    logistic = jax.nn.sigmoid(widened)
    activation = (widened * logistic).astype(jnp.bfloat16)
    slope_factor = logistic * (1.0 + widened * (1.0 - logistic))
    earlier = from_behind(activation[:, :, frames - 2 :, :], "tm", 1)
    extended = jnp.concatenate([earlier, activation], axis=2)
    upcoming = from_behind(cotangent[:, :, :2, :], "tm", -1)
    later_padded = jnp.concatenate([cotangent, upcoming], axis=2)
    cotangent_rows = cotangent.reshape(channels, -1)
    portion = lax.all_gather(extended, "chan", axis=0, tiled=True)
    out_sum = jnp.zeros((channels, flat_length), jnp.float32)
    amount = portion.shape[0]
    copies = padded_copies(portion)
    kernel_cols = kernel
    grad_parts = []
    for forward_temporal in range(3):
        stacked = stacked_taps(copies, forward_temporal, False, frames, pixels)
        weights = kernel_cols[:, 9 * forward_temporal : 9 * forward_temporal + 9, :].reshape(
            channels, 9 * amount
        )
        out_sum = out_sum + jnp.dot(weights, stacked, preferred_element_type=jnp.float32)
        grad_parts.append(
            lax.dot_general(
                cotangent_rows,
                stacked,
                (((1,), (1,)), ((), ())),
                preferred_element_type=jnp.float32,
            ).reshape(channels, 9, amount)
        )
    grad_sum = jnp.concatenate(grad_parts, axis=1)
    out_sum, grad_sum = (out_sum, grad_sum)
    conv_out = out_sum.reshape(features.shape).astype(jnp.bfloat16)
    position_count = lax.axis_size("dp") * lax.axis_size("tm") * flat_length
    kernel_grad = lax.psum(grad_sum, ("tm", "dp")) * (1.0 / math.sqrt(position_count))
    padded_later = padded_copies(later_padded)
    later_stacks = [
        stacked_taps(padded_later, 2 - temporal, True, frames, pixels) for temporal in range(3)
    ]
    amount = channels * lax.axis_size("chan")
    kernel_cols = kernel
    summed = jnp.zeros((amount, flat_length), jnp.float32)
    for temporal in range(3):
        weights = jnp.transpose(
            kernel_cols[:, 9 * temporal : 9 * temporal + 9, :], (2, 1, 0)
        ).reshape(amount, 9 * channels)
        summed = summed + jnp.dot(
            weights, later_stacks[temporal], preferred_element_type=jnp.float32
        )
    before_slope = lax.psum_scatter(
        summed.reshape(amount, clip_count, frames, pixels), "chan", scatter_dimension=0, tiled=True
    )
    feature_grad = (before_slope * slope_factor).astype(jnp.bfloat16)
    return (conv_out, feature_grad, kernel_grad)


def solution(mesh):
    return jax.shard_map(
        local,
        mesh=mesh,
        in_specs=(
            P("chan", ("groups", "dp"), "tm", None),
            P("chan", None, None),
            P("chan", ("groups", "dp"), "tm", None),
        ),
        out_specs=(
            P("chan", ("groups", "dp"), "tm", None),
            P("chan", ("groups", "dp"), "tm", None),
            P(("groups", "chan"), None, None),
        ),
        check_vma=False,
    )
```

profile of v0, /device:TPU:0, one launch (start us, length us, event | category | flops | bytes accessed | tf_op | source)
XLA Modules:
  0.0 263.4 jit_solution(15302708623575649266)
XLA Ops:
  7.2 1.0 slice.215
  8.2 1.4 collective-permute-start.1
  9.7 1.7 fusion.80
  11.6 0.3 broadcast_select_fusion.2
  13.0 0.5 fusion.67
  13.6 0.6 fusion.58
  14.8 0.3 fusion.50
  15.1 0.6 fusion.76
  16.5 0.5 fusion.64
  17.0 0.5 fusion.56
  17.5 0.5 fusion.73
  18.0 0.4 copy.33
  18.4 0.4 copy.34
  18.8 0.4 copy.35
  19.2 1.2 fusion.82
  20.4 1.2 fusion.83
  21.7 1.3 add_add_fusion
  23.0 1.6 copy.23
  24.7 38.9 %reduce-scatter.2.cloned.1.call-done = f32[96,1,4,256]{3,0,2,1:T(8,128)} async-done(((f32[384,1,4,256]{3,0,2,1:T(8,128)}), f32[96,1,4,256]{3,0,2,1:T(8,128)}) %reduce-scatter.2.cloned.1.call-update) | async-done | bytes 393232 | tf_op jit(solution)/shard_map/reduce_scatter | solution.py:99
  63.6 1.8 fusion.48
  65.4 1.4 collective-permute-start
  66.8 0.9 collective-permute-done
  67.7 0.7 pad_maximum_fusion.2
  68.7 29.4 %all-gather.2.cloned.1.call-done = bf16[384,1,6,256]{3,0,2,1:T(8,128)(2,1)} async-done(((bf16[96,1,6,256]{3,0,2,1:T(8,128)(2,1)}), bf16[384,1,6,256]{3,0,2,1:T(8,128)(2,1)}) %all-gather.2.cloned.1.call-update) | async-done | bytes 1179664 | tf_op jit(solution)/shard_map/all_gather | solution.py:60
  98.1 1.5 broadcast_select_fusion
  99.6 0.3 fusion.29
  99.9 0.3 fusion.21
  100.3 0.3 fusion.38
  100.6 0.6 fusion.30
  101.1 0.3 slice_dynamic-update-slice_fusion
  101.5 0.6 fusion.39
  102.1 1.7 fusion.31
  103.8 1.5 fusion.22
  105.3 1.7 fusion.40
  107.0 1.4 fusion.27
  108.5 1.6 slice_dynamic-update-slice_fusion.1
  110.1 1.2 fusion.36
  111.3 1.5 fusion.28
  112.7 1.5 fusion.20
  114.2 1.4 fusion.37
  115.7 2.9 %copy-done.1 = bf16[3456,1,4,256]{3,0,2,1:T(8,128)(2,1)} copy-done((bf16[3456,1,4,256]{3,0,2,1:T(8,128)(2,1)}, bf16[3456,1,4,256]{3,0,2,1:T(8,128)(2,1)S(1)}, u32[]{:S(2)}) %copy-start.1) | copy-done | bytes 7077912
  118.6 2.2 fusion.6
  120.8 0.5 copy.25
  121.4 5.2 %fusion.9 = f32[96,3456]{1,0:T(8,128)S(1)} fusion(bf16[3456,1,4,256]{3,0,2,1:T(8,128)(2,1)} %get-tuple-element.27, bf16[96,4,256]{2,1,0:T(4,128)(2,1)S(1)} %bitcast.81), kind=kOutput, calls=%fused_computation.26 | convolution fusion | flops 679477248 | bytes 8601600 | tf_op jit(solution)/shard_map/dot_general | solution.py:73
  126.6 1.8 copy.27
  128.4 6.3 %fusion.12 = f32[96,3456]{1,0:T(8,128)} fusion(bf16[3456,1,4,256]{3,0,2,1:T(8,128)(2,1)} %copy-done.2, bf16[96,4,256]{2,1,0:T(4,128)(2,1)S(1)} %bitcast.82), kind=kOutput, calls=%fused_computation.27 | convolution fusion | flops 679477248 | bytes 8601600 | tf_op jit(solution)/shard_map/dot_general | solution.py:73
  134.7 3.4 %copy.29 = f32[96,3456]{0,1:T(8,128)} copy(f32[96,3456]{1,0:T(8,128)} %fusion.12) | data formatting | bytes 2654208 | tf_op jit(solution)/shard_map/dot_general | solution.py:73
  138.1 4.3 %pad_maximum_fusion = f32[96,27,384]{0,2,1:T(8,128)} fusion(f32[96,9,384]{0,2,1:T(8,128)} %bitcast.85, f32[96,9,384]{0,2,1:T(8,128)S(1)} %bitcast.84, f32[96,9,384]{0,2,1:T(8,128)S(1)} %bitcast.83), kind=kLoop, calls=%fused_computation.6 | loop fusion | flops 1990656 | bytes 7962624 | tf_op jit(solution)/shard_map/concatenate | solution.py:80
  142.5 1.1 copy-done.11
  143.5 0.4 copy.18
  144.0 0.7 copy-done.9
  144.6 0.4 copy.20
  145.1 0.4 copy.22
  145.5 0.8 copy.31
  146.4 9.9 %copy.17 = bf16[3456,1,4,256]{0,3,2,1:T(8,128)(2,1)} copy(bf16[3456,1,4,256]{3,0,2,1:T(8,128)(2,1)} %copy-done.1) | data formatting | bytes 14155776 | tf_op jit(solution)/shard_map/concatenate | solution.py:44
  156.2 10.3 %copy.19 = bf16[3456,1,4,256]{0,3,2,1:T(8,128)(2,1)} copy(bf16[3456,1,4,256]{3,0,2,1:T(8,128)(2,1)} %get-tuple-element.27) | data formatting | bytes 14155776 | tf_op jit(solution)/shard_map/concatenate | solution.py:44
  166.6 9.7 %copy.21 = bf16[3456,1,4,256]{0,3,2,1:T(8,128)(2,1)} copy(bf16[3456,1,4,256]{3,0,2,1:T(8,128)(2,1)} %copy-done.2) | data formatting | bytes 14155776 | tf_op jit(solution)/shard_map/concatenate | solution.py:44
  176.3 5.5 %fusion.81 = f32[1024,96]{0,1:T(8,128)S(1)} fusion(bf16[3456,1024]{0,1:T(8,128)(2,1)} %bitcast.77, bf16[96,3456]{0,1:T(8,128)(2,1)S(1)} %bitcast.89), kind=kOutput, calls=%fused_computation.148 | convolution fusion | flops 679477248 | bytes 8134656 | tf_op jit(solution)/shard_map/dot_general | solution.py:71
  181.8 2.3 convolution_add_fusion.1
  184.1 2.3 fusion.16
  186.4 0.8 convert_element_type.38
  187.2 58.2 %all-reduce.8.cloned.1.call-done = f32[96,27,384]{0,2,1:T(8,128)} async-done(((f32[96,27,384]{0,2,1:T(8,128)}), f32[96,27,384]{0,2,1:T(8,128)}) %all-reduce.8.cloned.1.call-update) | async-done | bytes 3981328 | tf_op jit(solution)/shard_map/psum | solution.py:84
  245.5 5.4 %broadcast_multiply_fusion = f32[96,27,384]{0,2,1:T(8,128)} fusion(f32[96,27,384]{0,2,1:T(8,128)} %all-reduce.8.cloned.1.call-done), kind=kLoop, calls=%fused_computation.34 | loop fusion | flops 995328 | bytes 7962624 | tf_op jit(solution)/shard_map/mul | solution.py:84
  250.9 6.0 %copy.32 = f32[96,27,384]{2,0,1:T(8,128)} copy(f32[96,27,384]{0,2,1:T(8,128)} %broadcast_multiply_fusion) | data formatting | bytes 7962624
  (50 shorter events, 3.1 us)
Async XLA Ops:
  7.2 56.4 %reduce-scatter.2.cloned.1.call-start = ((), (), s32[]{:S(2)}) async-start(), calls=%async_computation.2 | async-start | bytes 1966080 | tf_op jit(solution)/shard_map/reduce_scatter | solution.py:99
  8.2 3.3 %copy-start.4 = (bf16[96,1,4,256]{3,2,1,0:T(4,128)(2,1)S(1)}, bf16[96,1,4,256]{3,2,1,0:T(4,128)(2,1)}, u32[]{:S(2)}) copy-start(bf16[96,1,4,256]{3,2,1,0:T(4,128)(2,1)} %param.5) | copy-start | bytes 589828
  8.2 3.3 %collective-permute-start.1 = (bf16[96,1,2,256]{3,2,1,0:T(2,128)(2,1)S(1)}, bf16[96,1,2,256]{3,2,1,0:T(2,128)(2,1)S(1)}, u32[]{:S(2)}, u32[]{:S(2)}) collective-permute-start(bf16[96,1,2,256]{3,2,1,0:T(2,128)(2,1)S(1)} %slice.215), channel_id=1, source_target_pairs={{2,0},{3,1},{6,4},{7,5},{10,8},{11,9},{14,12},{15,13},{18,16},{19,... | collective-permute-start | bytes 294920 | tf_op jit(solution)/shard_map/ppermute | solution.py:14
  11.4 7.8 %copy-start.10 = (bf16[96,9,384]{2,0,1:T(8,128)(2,1)}, bf16[96,9,384]{2,0,1:T(8,128)(2,1)S(1)}, u32[]{:S(2)}) copy-start(bf16[96,9,384]{2,0,1:T(8,128)(2,1)S(1)} %get-tuple-element.10) | copy-start | bytes 1990660
  11.4 9.0 %copy-start.8 = (bf16[96,9,384]{2,0,1:T(8,128)(2,1)}, bf16[96,9,384]{2,0,1:T(8,128)(2,1)S(1)}, u32[]{:S(2)}) copy-start(bf16[96,9,384]{2,0,1:T(8,128)(2,1)S(1)} %get-tuple-element.11) | copy-start | bytes 1990660
  11.4 10.3 %copy-start.6 = (bf16[96,9,384]{2,0,1:T(8,128)(2,1)}, bf16[96,9,384]{2,0,1:T(8,128)(2,1)S(1)}, u32[]{:S(2)}) copy-start(bf16[96,9,384]{2,0,1:T(8,128)(2,1)S(1)} %get-tuple-element.9) | copy-start | bytes 1990660
  23.0 40.6 %copy-start.13 = (bf16[96,1,4,256]{3,2,1,0:T(4,128)(2,1)S(1)}, bf16[96,1,4,256]{3,2,1,0:T(4,128)(2,1)}, u32[]{:S(2)}) copy-start(bf16[96,1,4,256]{3,2,1,0:T(4,128)(2,1)} %param.3) | copy-start | bytes 589828
  24.6 73.5 %all-gather.2.cloned.1.call-start = ((), (), s32[]{:S(2)}) async-start(), calls=%async_computation.1 | async-start | bytes 1474560 | tf_op jit(solution)/shard_map/all_gather | solution.py:60
  65.4 2.3 collective-permute-start
  68.5 177.0 %all-reduce.8.cloned.1.call-start = ((), (), s32[]{:S(2)}) async-start(), calls=%async_computation.3 | async-start | bytes 10616832 | tf_op jit(solution)/shard_map/psum | solution.py:84
  98.1 1.8 copy-start
  107.0 8.6 %copy-start.2 = (bf16[3456,1,4,256]{3,0,2,1:T(8,128)(2,1)}, bf16[3456,1,4,256]{3,0,2,1:T(8,128)(2,1)S(1)}, u32[]{:S(2)}) copy-start(bf16[3456,1,4,256]{3,0,2,1:T(8,128)(2,1)S(1)} %get-tuple-element.12) | copy-start | bytes 21233668
  115.7 2.9 %copy-start.1 = (bf16[3456,1,4,256]{3,0,2,1:T(8,128)(2,1)}, bf16[3456,1,4,256]{3,0,2,1:T(8,128)(2,1)S(1)}, u32[]{:S(2)}) copy-start(bf16[3456,1,4,256]{3,0,2,1:T(8,128)(2,1)S(1)} %get-tuple-element.28) | copy-start | bytes 21233668
  134.7 3.4 %copy-start.5 = (f32[96,3456]{0,1:T(8,128)S(1)}, f32[96,3456]{0,1:T(8,128)}, u32[]{:S(2)}) copy-start(f32[96,3456]{0,1:T(8,128)} %copy.27) | copy-start | bytes 3981316
  142.4 1.1 copy-start.11
  143.5 1.1 copy-start.9
  143.5 1.5 copy-start.7
  143.5 2.0 copy-start.12
  176.3 5.5 %copy-start.3 = (bf16[3456,1,4,256]{0,3,2,1:T(8,128)(2,1)S(1)}, bf16[3456,1,4,256]{0,3,2,1:T(8,128)(2,1)}, u32[]{:S(2)}) copy-start(bf16[3456,1,4,256]{0,3,2,1:T(8,128)(2,1)} %copy.19) | copy-start | bytes 21233668
  176.3 7.8 %slice-start = ((s8[7077888]{0:T(1024)(128)(4,1)}), s8[4194304]{0:T(1024)(128)(4,1)S(1)}, s32[]{:S(2)}) async-start(s8[7077888]{0:T(1024)(128)(4,1)} %bitcast.73), calls=%async_computation.4 | async-start | bytes 8388608
  181.8 2.3 slice-start.1
Sparse Core Ops, SparseCore 0:
  24.7 38.8 reduce-scatter.1
  68.6 29.4 all-gather.1
  142.6 102.8 all-reduce.7
where the time goes:
time: 265 us; the launch traced here: 263 us
  waiting for transfers between devices  128 us (48%)
  local copies, waits for them, and re-layouts  76.3 us (29%)
  matrix products  27.6 us (10%)
  other arithmetic  14.7 us (6%)
  between operations  14.1 us (5%)
  starting transfers between devices  3.09 us (1%)
    psum x1, waiting for transfers between devices, local(): lax.psum(grad_sum, ('tm', 'dp')) * (1.0 / math.sqrt(position_count))  58.2 us
    reduce_scatter x1, waiting for transfers between devices, local(): lax.psum_scatter(summed.reshape(amount, clip_count, frames, pixels), 'cha...  38.9 us
    concatenate x7, local copies, waits for them, and re-layouts, stacked_taps(): concatenated = jnp.concatenate(pieces, axis=0)  34.2 us
    unnamed x64, local copies, waits for them, and re-layouts  29.9 us
    all_gather x1, waiting for transfers between devices, local(): portion = lax.all_gather(extended, 'chan', axis=0, tiled=True)  29.4 us
    dot_general x3, matrix products, local(): lax.dot_general(cotangent_rows, stacked, (((1,), (1,)), ((), ())), prefer...  13.8 us
    dot_general x3, matrix products, local(): jnp.dot(weights, stacked, preferred_element_type=jnp.float32)  10 us
    dot_general x3, local copies, waits for them, and re-layouts, local(): lax.dot_general(cotangent_rows, stacked, (((1,), (1,)), ((), ())), prefer...  5.72 us
  transfers between devices with their start and end apart: 5, of which 5 were waited for; matrix products, arithmetic and copies ran while one was open for 17% of the time, Pallas kernels for 0%

commit v1 on v0

--- a/solution.py
+++ b/solution.py
@@ -1,8 +1,11 @@
+import functools
 import math
 
 import jax
 import jax.numpy as jnp
 from jax import lax
+from jax.experimental import pallas as pl
+from jax.experimental.pallas import tpu as pltpu
 from jax.sharding import PartitionSpec as P
 
 WID = 64
@@ -103,9 +106,318 @@
     return (conv_out, feature_grad, kernel_grad)
 
 
+def moved(x, rows, columns, pixels):
+    step = rows * WID + columns
+    place = lax.broadcasted_iota(jnp.int32, x.shape, len(x.shape) - 1)
+    row, column = place // WID + rows, place % WID + columns
+    out = x if step == 0 else pltpu.roll(x, (-step) % pixels, len(x.shape) - 1)
+    inside = None
+    if rows:
+        inside = (row >= 0) & (row < pixels // WID)
+    if columns:
+        within = (column >= 0) & (column < WID)
+        inside = within if inside is None else inside & within
+    return out if inside is None else jnp.where(inside, out, 0.0)
+
+
+def silu(x):
+    wide = x.astype(jnp.float32)
+    return wide * jax.nn.sigmoid(wide)
+
+
+def body(
+    sizes,
+    f_ref, w_ref, g_ref,
+    out_ref, fg_ref, kg_ref,
+    halo, stack, turned, gathered, act, part, share, half_out, half_in, sum_out, sum_in, taps, edge_out, edge_in,
+    gather_send, gather_recv, halo_send, halo_recv, share_send, share_recv,
+    half_send, half_recv, sum_send, sum_recv, done_send, done_recv, edge_send, edge_recv,
+):
+    n, tm, scale = sizes
+    frames, c, pixels = f_ref.shape
+    full = c * n
+    half = c // 2
+    long = frames * pixels
+    z, t, d = lax.axis_index("chan"), lax.axis_index("tm"), lax.axis_index("dp")
+
+    def remote(src, dst, send, recv, **where):
+        return pltpu.make_async_remote_copy(
+            src_ref=src, dst_ref=dst, send_sem=send, recv_sem=recv,
+            device_id=where, device_id_type=pl.DeviceIdType.MESH,
+        )
+
+    barrier = pltpu.get_barrier_semaphore()
+    for k in range(1, n):
+        pl.semaphore_signal(barrier, inc=1, device_id={"chan": lax.rem(z + k, n)}, device_id_type=pl.DeviceIdType.MESH)
+    pl.semaphore_signal(barrier, inc=1, device_id={"tm": 1 - t}, device_id_type=pl.DeviceIdType.MESH)
+    pl.semaphore_signal(barrier, inc=1, device_id={"dp": 1 - d}, device_id_type=pl.DeviceIdType.MESH)
+    pl.semaphore_wait(barrier, n + 1)
+
+    def gather_to(k):
+        return remote(
+            f_ref, gathered.at[k - 1], gather_send.at[k - 1], gather_recv.at[k - 1], chan=lax.rem(z + k, n)
+        )
+
+    def halo_copy():
+        return remote(g_ref.at[pl.ds(0, 2)], halo, halo_send, halo_recv, tm=1 - t)
+
+    @pl.when(t == 1)
+    def _():
+        halo_copy().start()
+
+    for k in range(1, n):
+        gather_to(k).start()
+
+    def stack_frame(x, s):
+        wide = x.astype(jnp.float32)
+        for i in range(3):
+            for j in range(3):
+                stack[3 * i + j, :, pl.ds(pl.multiple_of(s * pixels, pixels), pixels)] = moved(
+                    wide, 1 - i, 1 - j, pixels
+                ).astype(jnp.bfloat16)
+
+    def own_frame(s, _):
+        stack_frame(g_ref[s], s)
+        return 0
+
+    lax.fori_loop(0, frames, own_frame, 0)
+
+    @pl.when(t == 0)
+    def _():
+        halo_copy().wait_recv()
+
+        def next_frame(s, _):
+            stack_frame(halo[s], frames + s)
+            return 0
+
+        lax.fori_loop(0, 2, next_frame, 0)
+
+    @pl.when(t == 1)
+    def _():
+        stack[:, :, long : long + 2 * pixels] = jnp.zeros((9, c, 2 * pixels), jnp.bfloat16)
+        halo_copy().wait_send()
+
+    def turn(a, _):
+        turned[a] = jnp.transpose(w_ref[pl.ds(9 * a, 9)].reshape(9 * c, full))
+        return 0
+
+    lax.fori_loop(0, 3, turn, 0)
+
+    def share_to(k, s):
+        peer = lax.rem(z + k, n)
+        return remote(
+            part.at[s, pl.ds(pl.multiple_of(peer * c, c), c)], share.at[k - 1, s],
+            share_send.at[k - 1, s], share_recv.at[k - 1, s], chan=peer,
+        )
+
+    def before(s, _):
+        total = jnp.zeros((full, pixels), jnp.float32)
+        for a in range(3):
+            lanes = pl.ds(pl.multiple_of((s + 2 - a) * pixels, pixels), pixels)
+            total = total + jnp.dot(
+                turned[a], stack[:, :, lanes].reshape(9 * c, pixels), preferred_element_type=jnp.float32
+            )
+        part[s] = total.astype(jnp.bfloat16)
+        for k in range(1, n):
+            share_to(k, s).start()
+        return 0
+
+    lax.fori_loop(0, frames, before, 0)
+
+    for k in range(n):
+        origin = pl.ds(pl.multiple_of(lax.rem(z + n - k, n) * c, c), c)
+        if k:
+            gather_to(k).wait_recv()
+        for s in range(frames):
+            block = gathered[k - 1, s] if k else f_ref[s]
+            act[origin, s * pixels : (s + 1) * pixels] = silu(block).astype(jnp.bfloat16)
+
+    def half_rows(which):
+        return pl.ds(pl.multiple_of(which * half, half), half)
+
+    def half_copy(a):
+        return remote(half_out.at[a], half_in.at[a], half_send.at[a], half_recv.at[a], tm=1 - t)
+
+    def sum_copy(a):
+        return remote(sum_out.at[a], sum_in.at[a], sum_send.at[a], sum_recv.at[a], dp=1 - d)
+
+    def kernel_terms(a, which):
+        lanes = pl.ds(pl.multiple_of((2 - a) * pixels, pixels), long)
+        rows = stack[:, half_rows(which), lanes].reshape(9 * half, long)
+        return lax.dot_general(
+            rows, act[...], (((1,), (1,)), ((), ())), preferred_element_type=jnp.float32
+        ).reshape(9, half, full)
+
+    def terms(a, _):
+        half_out[a] = kernel_terms(a, 1 - t).astype(jnp.bfloat16)
+        half_copy(a).start()
+        mine = kernel_terms(a, t)
+        half_copy(a).wait_recv()
+        sum_out[a] = (mine + half_in[a].astype(jnp.float32)).astype(jnp.bfloat16)
+        sum_copy(a).start()
+        return 0
+
+    lax.fori_loop(0, 3, terms, 0)
+
+    def edge_copy():
+        return remote(edge_out, edge_in, edge_send, edge_recv, tm=1 - t)
+
+    def convolved(u):
+        total = None
+        for a in range(3):
+            s = u + a - 2
+            if 0 <= s < frames:
+                term = jnp.dot(
+                    w_ref[9 * a : 9 * a + 9].reshape(9 * c, full),
+                    act[:, s * pixels : (s + 1) * pixels],
+                    preferred_element_type=jnp.float32,
+                )
+                total = term if total is None else total + term
+        taps[...] = total.reshape(9, c, pixels)
+        result = jnp.zeros((c, pixels), jnp.float32)
+        for i in range(3):
+            for j in range(3):
+                result = result + moved(taps[3 * i + j], i - 1, j - 1, pixels)
+        return result
+
+    @pl.when(t == 0)
+    def _():
+        for u in range(2):
+            edge_out[u] = convolved(frames + u)
+        edge_copy().start()
+
+    for u in list(range(2, frames)):
+        out_ref[u] = convolved(u).astype(jnp.bfloat16)
+    for u in range(2):
+        taps_sum = convolved(u)
+
+        @pl.when(t == 0)
+        def _():
+            out_ref[u] = taps_sum.astype(jnp.bfloat16)
+
+        @pl.when(t == 1)
+        def _():
+            if u == 0:
+                edge_copy().wait_recv()
+            out_ref[u] = (taps_sum + edge_in[u]).astype(jnp.bfloat16)
+
+    def done_copy(a):
+        place = kg_ref.at[pl.ds(9 * a, 9), half_rows(t)]
+        return remote(place, place, done_send.at[a], done_recv.at[a], tm=1 - t)
+
+    def finish(a, _):
+        sum_copy(a).wait_recv()
+        kg_ref[pl.ds(9 * a, 9), half_rows(t)] = (
+            sum_out[a].astype(jnp.float32) + sum_in[a].astype(jnp.float32)
+        ) * scale
+        done_copy(a).start()
+        return 0
+
+    lax.fori_loop(0, 3, finish, 0)
+
+    def slope_frame(s, _):
+        total = part[s, pl.ds(pl.multiple_of(z * c, c), c)].astype(jnp.float32)
+        for k in range(1, n):
+            share_to(k, s).wait_recv()
+            total = total + share[k - 1, s].astype(jnp.float32)
+        wide = f_ref[s].astype(jnp.float32)
+        logistic = jax.nn.sigmoid(wide)
+        fg_ref[s] = (total * (logistic * (1.0 + wide * (1.0 - logistic)))).astype(jnp.bfloat16)
+        return 0
+
+    lax.fori_loop(0, frames, slope_frame, 0)
+
+    def drain_shares(s, _):
+        for k in range(1, n):
+            share_to(k, s).wait_send()
+        return 0
+
+    lax.fori_loop(0, frames, drain_shares, 0)
+    for k in range(1, n):
+        gather_to(k).wait_send()
+
+    @pl.when(t == 0)
+    def _():
+        edge_copy().wait_send()
+
+    def drain_terms(a, _):
+        half_copy(a).wait_send()
+        sum_copy(a).wait_send()
+        done_copy(a).wait()
+        return 0
+
+    lax.fori_loop(0, 3, drain_terms, 0)
+
+
+def fits(mesh, features, kernel):
+    c, clips, frames, pixels = features.shape
+    return (
+        mesh.shape["tm"] == 2
+        and mesh.shape["dp"] == 2
+        and clips == 1
+        and frames >= 2
+        and c % 32 == 0
+        and kernel.shape[2] % 128 == 0
+        and pixels % 128 == 0
+        and pixels % WID == 0
+        and c * mesh.shape["chan"] == kernel.shape[2]
+        and kernel.size * 14 + features.size * 64 < 48 * 2**20
+    )
+
+
+def fused(mesh, features, kernel, cotangent):
+    c, clips, frames, pixels = features.shape
+    n = mesh.shape["chan"]
+    full = c * n
+    scale = 1.0 / math.sqrt(mesh.shape["dp"] * mesh.shape["tm"] * clips * frames * pixels)
+    by_frame = lambda x: jnp.transpose(x.reshape(c, frames, pixels), (1, 0, 2))
+    back = lambda x: jnp.transpose(x, (1, 0, 2)).reshape(c, clips, frames, pixels)
+    vmem = pl.BlockSpec(memory_space=pltpu.VMEM)
+    b16, f32 = jnp.bfloat16, jnp.float32
+    dma = pltpu.SemaphoreType.DMA
+    half = c // 2
+    halves = pltpu.VMEM((3, 9, half, full), b16)
+    conv_out, feature_grad, kernel_grad = pl.pallas_call(
+        functools.partial(body, (n, mesh.shape["tm"], scale)),
+        out_shape=(
+            jax.ShapeDtypeStruct((frames, c, pixels), b16),
+            jax.ShapeDtypeStruct((frames, c, pixels), b16),
+            jax.ShapeDtypeStruct((27, c, full), f32),
+        ),
+        in_specs=[vmem] * 3,
+        out_specs=(vmem,) * 3,
+        scratch_shapes=[
+            pltpu.VMEM((2, c, pixels), b16),
+            pltpu.VMEM((9, c, (frames + 2) * pixels), b16),
+            pltpu.VMEM((3, full, 9 * c), b16),
+            pltpu.VMEM((n - 1, frames, c, pixels), b16),
+            pltpu.VMEM((full, frames * pixels), b16),
+            pltpu.VMEM((frames, full, pixels), b16),
+            pltpu.VMEM((n - 1, frames, c, pixels), b16),
+            halves, halves, halves, halves,
+            pltpu.VMEM((9, c, pixels), f32),
+            pltpu.VMEM((2, c, pixels), f32),
+            pltpu.VMEM((2, c, pixels), f32),
+            dma((n - 1,)), dma((n - 1,)), dma, dma,
+            dma((n - 1, frames)), dma((n - 1, frames)),
+            dma((3,)), dma((3,)), dma((3,)), dma((3,)), dma((3,)), dma((3,)), dma, dma,
+        ],
+        compiler_params=pltpu.CompilerParams(
+            collective_id=0, has_side_effects=True, vmem_limit_bytes=56 * 2**20
+        ),
+        name="video_conv",
+    )(by_frame(features), jnp.transpose(kernel, (1, 0, 2)), by_frame(cotangent))
+    return back(conv_out), back(feature_grad), jnp.transpose(kernel_grad, (1, 0, 2))
+
+
 def solution(mesh):
+    def chosen(features, kernel, cotangent):
+        if fits(mesh, features, kernel):
+            return fused(mesh, features, kernel, cotangent)
+        return local(features, kernel, cotangent)
+
     return jax.shard_map(
-        local,
+        chosen,
         mesh=mesh,
         in_specs=(
             P("chan", ("groups", "dp"), "tm", None),

time: 265 us -> 72.3 us (0.27)
  the two profiles are of different devices: /device:TPU:0 before, /device:TPU:25 now
where the time goes in v1:
time: 72.3 us; the launch traced here: 72 us
  Pallas kernels  61.8 us (85%)
  local copies, waits for them, and re-layouts  9.64 us (13%)
    pallas_call x1, Pallas kernels, fused(): pl.pallas_call(functools.partial(body, (n, mesh.shape['tm'], scale)), out...  61.8 us
    unnamed x3, local copies, waits for them, and re-layouts  7.84 us
    transpose x1, local copies, waits for them, and re-layouts, fused(): by_frame = lambda x: jnp.transpose(x.reshape(c, frames, pixels), (1, 0, 2))  1.8 us

profile of v1, /device:TPU:25, one launch (start us, length us, event | category | flops | bytes accessed | tf_op | source)
XLA Modules:
  0.0 72.0 jit_solution(13543991182311320437)
XLA Ops:
  0.6 1.8 %copy_bitcast_fusion = (bf16[4,96,256]{2,1,0:T(8,128)(2,1)}, bf16[4,96,256]{2,1,0:T(8,128)(2,1)}) fusion(bf16[96,1,4,256]{3,2,1,0:T(4,128)(2,1)} %param.5, bf16[96,1,4,256]{3,2,1,0:T(4,128)(2,1)} %param.3), kind=kLoop, calls=%fused_computation | loop fusion | bytes 786432 | tf_op jit(solution)/shard_map/transpose | solution.py:373
  2.4 61.8 %video_conv.1 = (bf16[4,96,256]{2,1,0:T(8,128)(2,1)}, bf16[4,96,256]{2,1,0:T(8,128)(2,1)}, f32[27,96,384]{2,1,0:T(8,128)}) custom-call(bf16[4,96,256]{2,1,0:T(8,128)(2,1)} %get-tuple-element.13.f_ref, bf16[27,96,384]{2,1,0:T(8,128)(2,1)} %bitcast.17, bf16[4,96,256]{2,1,0:T(8,128)(2,1)} %get-tuple-element.12.g_ref), custom_call_target="tpu_custom_call" | custom-call | tf_op jit(solution)/shard_map/video_conv/pallas_call | solution.py:380
  64.2 1.8 %copy.8 = bf16[96,1,4,256]{3,2,1,0:T(4,128)(2,1)} copy(bf16[96,1,4,256]{3,0,2,1:T(8,128)(2,1)} %bitcast.19) | data formatting | bytes 393216
  66.0 1.8 %copy.9 = bf16[96,1,4,256]{3,2,1,0:T(4,128)(2,1)} copy(bf16[96,1,4,256]{3,0,2,1:T(8,128)(2,1)} %bitcast.18) | data formatting | bytes 393216
  67.7 4.3 %copy.13 = f32[96,27,384]{2,0,1:T(8,128)} copy(f32[96,27,384]{2,0,1:T(8,128)} %bitcast.16) | data formatting | bytes 7962624

commit v2 on v1

--- a/solution.py
+++ b/solution.py
@@ -129,15 +129,16 @@
     sizes,
     f_ref, w_ref, g_ref,
     out_ref, fg_ref, kg_ref,
-    halo, stack, turned, gathered, act, part, share, half_out, half_in, sum_out, sum_in, taps, edge_out, edge_in,
-    gather_send, gather_recv, halo_send, halo_recv, share_send, share_recv,
+    halo, stack, turned, gathered, act, part, right_in, left_in, half_out, half_in, sum_out, sum_in, taps, edge_out, edge_in,
+    gather_right, gather_left, gather_recv, halo_send, halo_recv, right_send, right_recv, left_send, left_recv,
     half_send, half_recv, sum_send, sum_recv, done_send, done_recv, edge_send, edge_recv,
 ):
-    n, tm, scale = sizes
+    n, lanes = sizes
     frames, c, pixels = f_ref.shape
     full = c * n
     half = c // 2
     long = frames * pixels
+    groups = full // lanes
     z, t, d = lax.axis_index("chan"), lax.axis_index("tm"), lax.axis_index("dp")
 
     def remote(src, dst, send, recv, **where):
@@ -147,26 +148,49 @@
         )
 
     barrier = pltpu.get_barrier_semaphore()
+
+    def greet(**where):
+        pl.semaphore_signal(barrier, inc=1, device_id=where, device_id_type=pl.DeviceIdType.MESH)
+
+    greet(tm=1 - t)
+    greet(dp=1 - d)
+
     for k in range(1, n):
-        pl.semaphore_signal(barrier, inc=1, device_id={"chan": lax.rem(z + k, n)}, device_id_type=pl.DeviceIdType.MESH)
-    pl.semaphore_signal(barrier, inc=1, device_id={"tm": 1 - t}, device_id_type=pl.DeviceIdType.MESH)
-    pl.semaphore_signal(barrier, inc=1, device_id={"dp": 1 - d}, device_id_type=pl.DeviceIdType.MESH)
+        greet(chan=lax.rem(z + k, n))
     pl.semaphore_wait(barrier, n + 1)
 
-    def gather_to(k):
-        return remote(
-            f_ref, gathered.at[k - 1], gather_send.at[k - 1], gather_recv.at[k - 1], chan=lax.rem(z + k, n)
-        )
+    def shard(q):
+        return gathered.at[q]
+
+    def pass_right(k):
+        q = z - k
+        return remote(f_ref if k == 0 else shard(q), shard(q), gather_right.at[k], gather_recv.at[q], chan=z + 1)
+
+    def pass_left(k):
+        q = z + k
+        return remote(f_ref if k == 0 else shard(q), shard(q), gather_left.at[k], gather_recv.at[q], chan=z - 1)
+
+    def arrival(q):
+        return remote(shard(q), shard(q), gather_right.at[0], gather_recv.at[q], chan=lax.rem(z + 1, n))
 
     def halo_copy():
         return remote(g_ref.at[pl.ds(0, 2)], halo, halo_send, halo_recv, tm=1 - t)
 
+    @pl.when(z < n - 1)
+    def _():
+        pass_right(0).start()
+
+    @pl.when(z > 0)
+    def _():
+        pass_left(0).start()
+
     @pl.when(t == 1)
     def _():
         halo_copy().start()
 
-    for k in range(1, n):
-        gather_to(k).start()
+    def activate(block, q):
+        for s in range(frames):
+            act[pl.ds(pl.multiple_of(q * c, c), c), s * pixels : (s + 1) * pixels] = silu(block[s]).astype(jnp.bfloat16)
 
     def stack_frame(x, s):
         wide = x.astype(jnp.float32)
@@ -197,67 +221,139 @@
         stack[:, :, long : long + 2 * pixels] = jnp.zeros((9, c, 2 * pixels), jnp.bfloat16)
         halo_copy().wait_send()
 
+    activate(f_ref, z)
+
     def turn(a, _):
         turned[a] = jnp.transpose(w_ref[pl.ds(9 * a, 9)].reshape(9 * c, full))
         return 0
 
     lax.fori_loop(0, 3, turn, 0)
 
-    def share_to(k, s):
-        peer = lax.rem(z + k, n)
-        return remote(
-            part.at[s, pl.ds(pl.multiple_of(peer * c, c), c)], share.at[k - 1, s],
-            share_send.at[k - 1, s], share_recv.at[k - 1, s], chan=peer,
-        )
+    def arrive(k):
+        @pl.when(z >= k)
+        def _():
+            arrival(z - k).wait_recv()
+
+            @pl.when(z < n - 1)
+            def _():
+                pass_right(k).start()
+
+        @pl.when(z + k < n)
+        def _():
+            arrival(z + k).wait_recv()
+
+            @pl.when(z > 0)
+            def _():
+                pass_left(k).start()
+
+        @pl.when(z >= k)
+        def _():
+            activate(shard(z - k), z - k)
+
+        @pl.when(z + k < n)
+        def _():
+            activate(shard(z + k), z + k)
+
+    def half_rows(which):
+        return pl.ds(pl.multiple_of(which * half, half), half)
+
+    def group_at(i):
+        return pl.ds(pl.multiple_of((i + (2 * z // n) * (groups - 1 - 2 * i)) * lanes, lanes), lanes)
+
+    def half_copy(m):
+        return remote(half_out.at[m], half_in.at[m], half_send.at[m], half_recv.at[m], tm=1 - t)
+
+    def sum_copy(m):
+        return remote(sum_out.at[m], sum_in.at[m], sum_send.at[m], sum_recv.at[m], dp=1 - d)
+
+    def kernel_terms(i, a, which):
+        span = pl.ds(pl.multiple_of((2 - a) * pixels, pixels), long)
+        rows = stack[:, half_rows(which), span].reshape(9 * half, long)
+        return lax.dot_general(
+            rows, act[group_at(i), :], (((1,), (1,)), ((), ())), preferred_element_type=jnp.float32
+        ).reshape(9, half, lanes)
+
+    def group_terms(i):
+        def theirs(a, _):
+            half_out[3 * i + a] = kernel_terms(i, a, 1 - t).astype(jnp.bfloat16)
+            half_copy(3 * i + a).start()
+            return 0
+
+        lax.fori_loop(0, 3, theirs, 0)
+
+        def ours(a, _):
+            m = 3 * i + a
+            mine = kernel_terms(i, a, t)
+            half_copy(m).wait_recv()
+            sum_out[m] = (mine + half_in[m].astype(jnp.float32)).astype(jnp.bfloat16)
+            sum_copy(m).start()
+            return 0
+
+        lax.fori_loop(0, 3, ours, 0)
+
+    def share_right(q, src):
+        return remote(src.at[q], right_in.at[q], right_send.at[q], right_recv.at[q], chan=z + 1)
+
+    def share_left(q, src):
+        return remote(src.at[q], left_in.at[q], left_send.at[q], left_recv.at[q], chan=z - 1)
 
     def before(s, _):
         total = jnp.zeros((full, pixels), jnp.float32)
         for a in range(3):
-            lanes = pl.ds(pl.multiple_of((s + 2 - a) * pixels, pixels), pixels)
+            span = pl.ds(pl.multiple_of((s + 2 - a) * pixels, pixels), pixels)
             total = total + jnp.dot(
-                turned[a], stack[:, :, lanes].reshape(9 * c, pixels), preferred_element_type=jnp.float32
+                turned[a], stack[:, :, span].reshape(9 * c, pixels), preferred_element_type=jnp.float32
             )
-        part[s] = total.astype(jnp.bfloat16)
-        for k in range(1, n):
-            share_to(k, s).start()
+        for q in range(n):
+            part[q, s] = total[q * c : (q + 1) * c].astype(jnp.bfloat16)
         return 0
 
-    lax.fori_loop(0, frames, before, 0)
-
-    for k in range(n):
-        origin = pl.ds(pl.multiple_of(lax.rem(z + n - k, n) * c, c), c)
-        if k:
-            gather_to(k).wait_recv()
+    def add_part(held, q):
         for s in range(frames):
-            block = gathered[k - 1, s] if k else f_ref[s]
-            act[origin, s * pixels : (s + 1) * pixels] = silu(block).astype(jnp.bfloat16)
-
-    def half_rows(which):
-        return pl.ds(pl.multiple_of(which * half, half), half)
-
-    def half_copy(a):
-        return remote(half_out.at[a], half_in.at[a], half_send.at[a], half_recv.at[a], tm=1 - t)
-
-    def sum_copy(a):
-        return remote(sum_out.at[a], sum_in.at[a], sum_send.at[a], sum_recv.at[a], dp=1 - d)
-
-    def kernel_terms(a, which):
-        lanes = pl.ds(pl.multiple_of((2 - a) * pixels, pixels), long)
-        rows = stack[:, half_rows(which), lanes].reshape(9 * half, long)
-        return lax.dot_general(
-            rows, act[...], (((1,), (1,)), ((), ())), preferred_element_type=jnp.float32
-        ).reshape(9, half, full)
-
-    def terms(a, _):
-        half_out[a] = kernel_terms(a, 1 - t).astype(jnp.bfloat16)
-        half_copy(a).start()
-        mine = kernel_terms(a, t)
-        half_copy(a).wait_recv()
-        sum_out[a] = (mine + half_in[a].astype(jnp.float32)).astype(jnp.bfloat16)
-        sum_copy(a).start()
-        return 0
-
-    lax.fori_loop(0, 3, terms, 0)
+            held[q, s] = (held[q, s].astype(jnp.float32) + part[q, s].astype(jnp.float32)).astype(jnp.bfloat16)
+
+    def first_shares():
+        for j in range(n - 1):
+            @pl.when(z == 0)
+            def _():
+                share_right(n - 1 - j, part).start()
+
+            @pl.when(z == n - 1)
+            def _():
+                share_left(j, part).start()
+
+    def wait_share(held, q, sem):
+        remote(held.at[q], held.at[q], right_send.at[q], sem.at[q], chan=lax.rem(z + 1, n)).wait_recv()
+
+    def relay(j):
+        @pl.when((z > 0) & (z < n - 1 - j))
+        def _():
+            wait_share(right_in, n - 1 - j, right_recv)
+            add_part(right_in, n - 1 - j)
+            share_right(n - 1 - j, right_in).start()
+
+        @pl.when((z < n - 1) & (z > j))
+        def _():
+            wait_share(left_in, j, left_recv)
+            add_part(left_in, j)
+            share_left(j, left_in).start()
+
+    def ready_after(i):
+        first, last = i * lanes // c, ((i + 1) * lanes - 1) // c
+        return max(max(abs(at - first), abs(at - last)) for at in range((n + 1) // 2))
+
+    arrived = 0
+    for i in range(groups):
+        while arrived < ready_after(i):
+            arrived += 1
+            arrive(arrived)
+        group_terms(i)
+        if i == 0:
+            lax.fori_loop(0, frames, before, 0)
+            first_shares()
+    while arrived < n - 1:
+        arrived += 1
+        arrive(arrived)
 
     def edge_copy():
         return remote(edge_out, edge_in, edge_send, edge_recv, tm=1 - t)
@@ -280,79 +376,125 @@
                 result = result + moved(taps[3 * i + j], i - 1, j - 1, pixels)
         return result
 
+    relay(0)
+
     @pl.when(t == 0)
     def _():
         for u in range(2):
             edge_out[u] = convolved(frames + u)
         edge_copy().start()
 
-    for u in list(range(2, frames)):
-        out_ref[u] = convolved(u).astype(jnp.bfloat16)
-    for u in range(2):
-        taps_sum = convolved(u)
-
-        @pl.when(t == 0)
-        def _():
-            out_ref[u] = taps_sum.astype(jnp.bfloat16)
-
-        @pl.when(t == 1)
-        def _():
-            if u == 0:
-                edge_copy().wait_recv()
-            out_ref[u] = (taps_sum + edge_in[u]).astype(jnp.bfloat16)
-
-    def done_copy(a):
-        place = kg_ref.at[pl.ds(9 * a, 9), half_rows(t)]
-        return remote(place, place, done_send.at[a], done_recv.at[a], tm=1 - t)
-
-    def finish(a, _):
-        sum_copy(a).wait_recv()
-        kg_ref[pl.ds(9 * a, 9), half_rows(t)] = (
-            sum_out[a].astype(jnp.float32) + sum_in[a].astype(jnp.float32)
-        ) * scale
-        done_copy(a).start()
-        return 0
-
-    lax.fori_loop(0, 3, finish, 0)
+    later = list(range(2, frames)) + [0, 1]
+    for step, u in enumerate(later):
+        value = convolved(u)
+        if u >= 2:
+            out_ref[u] = value.astype(jnp.bfloat16)
+        else:
+            @pl.when(t == 0)
+            def _():
+                out_ref[u] = value.astype(jnp.bfloat16)
+
+            @pl.when(t == 1)
+            def _():
+                if u == 0:
+                    edge_copy().wait_recv()
+                out_ref[u] = (value + edge_in[u]).astype(jnp.bfloat16)
+        if step + 1 < n - 1:
+            relay(step + 1)
+    for j in range(len(later) + 1, n - 1):
+        relay(j)
+
+    def done_copy(i, a):
+        place = kg_ref.at[pl.ds(9 * a, 9), half_rows(t), group_at(i)]
+        return remote(place, place, done_send.at[3 * i + a], done_recv.at[3 * i + a], tm=1 - t)
+
+    def finish(i):
+        def one(a, _):
+            m = 3 * i + a
+            sum_copy(m).wait_recv()
+            kg_ref[pl.ds(9 * a, 9), half_rows(t), group_at(i)] = (
+                sum_out[m].astype(jnp.float32) + sum_in[m].astype(jnp.float32)
+            ).astype(jnp.bfloat16)
+            done_copy(i, a).start()
+            return 0
+
+        lax.fori_loop(0, 3, one, 0)
+
+    for i in range(groups - 1):
+        finish(i)
+
+    @pl.when(z > 0)
+    def _():
+        wait_share(right_in, z, right_recv)
+
+    @pl.when(z < n - 1)
+    def _():
+        wait_share(left_in, z, left_recv)
 
     def slope_frame(s, _):
-        total = part[s, pl.ds(pl.multiple_of(z * c, c), c)].astype(jnp.float32)
-        for k in range(1, n):
-            share_to(k, s).wait_recv()
-            total = total + share[k - 1, s].astype(jnp.float32)
         wide = f_ref[s].astype(jnp.float32)
         logistic = jax.nn.sigmoid(wide)
-        fg_ref[s] = (total * (logistic * (1.0 + wide * (1.0 - logistic)))).astype(jnp.bfloat16)
+        slope = logistic * (1.0 + wide * (1.0 - logistic))
+
+        def keep(total):
+            fg_ref[s] = (total * slope).astype(jnp.bfloat16)
+
+        own = part[z, s].astype(jnp.float32)
+
+        @pl.when(z == 0)
+        def _():
+            keep(own + left_in[z, s].astype(jnp.float32))
+
+        @pl.when(z == n - 1)
+        def _():
+            keep(own + right_in[z, s].astype(jnp.float32))
+
+        @pl.when((z > 0) & (z < n - 1))
+        def _():
+            keep(own + (left_in[z, s].astype(jnp.float32) + right_in[z, s].astype(jnp.float32)))
+
         return 0
 
     lax.fori_loop(0, frames, slope_frame, 0)
-
-    def drain_shares(s, _):
-        for k in range(1, n):
-            share_to(k, s).wait_send()
-        return 0
-
-    lax.fori_loop(0, frames, drain_shares, 0)
-    for k in range(1, n):
-        gather_to(k).wait_send()
+    finish(groups - 1)
+
+    for k in range(n - 1):
+        @pl.when((z < n - 1) & (z >= k))
+        def _():
+            pass_right(k).wait_send()
+
+        @pl.when((z > 0) & (z + k < n))
+        def _():
+            pass_left(k).wait_send()
+
+    for j in range(n - 1):
+        @pl.when(z < n - 1 - j)
+        def _():
+            share_right(n - 1 - j, right_in).wait_send()
+
+        @pl.when(z > j)
+        def _():
+            share_left(j, left_in).wait_send()
 
     @pl.when(t == 0)
     def _():
         edge_copy().wait_send()
 
-    def drain_terms(a, _):
-        half_copy(a).wait_send()
-        sum_copy(a).wait_send()
-        done_copy(a).wait()
-        return 0
-
-    lax.fori_loop(0, 3, drain_terms, 0)
+    for i in range(groups):
+        def drain(a, _):
+            half_copy(3 * i + a).wait_send()
+            sum_copy(3 * i + a).wait_send()
+            done_copy(i, a).wait()
+            return 0
+
+        lax.fori_loop(0, 3, drain, 0)
 
 
 def fits(mesh, features, kernel):
     c, clips, frames, pixels = features.shape
     return (
         mesh.shape["tm"] == 2
+        and mesh.shape["chan"] >= 2
         and mesh.shape["dp"] == 2
         and clips == 1
         and frames >= 2
@@ -376,13 +518,16 @@
     b16, f32 = jnp.bfloat16, jnp.float32
     dma = pltpu.SemaphoreType.DMA
     half = c // 2
-    halves = pltpu.VMEM((3, 9, half, full), b16)
+    lanes = 128
+    pieces = 3 * (full // lanes)
+    halves = pltpu.VMEM((pieces, 9, half, lanes), b16)
+    shards = pltpu.VMEM((n, frames, c, pixels), b16)
     conv_out, feature_grad, kernel_grad = pl.pallas_call(
-        functools.partial(body, (n, mesh.shape["tm"], scale)),
+        functools.partial(body, (n, lanes)),
         out_shape=(
             jax.ShapeDtypeStruct((frames, c, pixels), b16),
             jax.ShapeDtypeStruct((frames, c, pixels), b16),
-            jax.ShapeDtypeStruct((27, c, full), f32),
+            jax.ShapeDtypeStruct((27, c, full), b16),
         ),
         in_specs=[vmem] * 3,
         out_specs=(vmem,) * 3,
@@ -390,24 +535,24 @@
             pltpu.VMEM((2, c, pixels), b16),
             pltpu.VMEM((9, c, (frames + 2) * pixels), b16),
             pltpu.VMEM((3, full, 9 * c), b16),
-            pltpu.VMEM((n - 1, frames, c, pixels), b16),
+            shards,
             pltpu.VMEM((full, frames * pixels), b16),
-            pltpu.VMEM((frames, full, pixels), b16),
-            pltpu.VMEM((n - 1, frames, c, pixels), b16),
+            shards, shards, shards,
             halves, halves, halves, halves,
             pltpu.VMEM((9, c, pixels), f32),
             pltpu.VMEM((2, c, pixels), f32),
             pltpu.VMEM((2, c, pixels), f32),
-            dma((n - 1,)), dma((n - 1,)), dma, dma,
-            dma((n - 1, frames)), dma((n - 1, frames)),
-            dma((3,)), dma((3,)), dma((3,)), dma((3,)), dma((3,)), dma((3,)), dma, dma,
+            dma((n,)), dma((n,)), dma((n,)), dma, dma,
+            dma((n,)), dma((n,)), dma((n,)), dma((n,)),
+            dma((pieces,)), dma((pieces,)), dma((pieces,)), dma((pieces,)), dma((pieces,)), dma((pieces,)), dma, dma,
         ],
         compiler_params=pltpu.CompilerParams(
             collective_id=0, has_side_effects=True, vmem_limit_bytes=56 * 2**20
         ),
         name="video_conv",
     )(by_frame(features), jnp.transpose(kernel, (1, 0, 2)), by_frame(cotangent))
-    return back(conv_out), back(feature_grad), jnp.transpose(kernel_grad, (1, 0, 2))
+    kernel_grad = jnp.transpose(kernel_grad, (1, 0, 2)).astype(f32) * scale
+    return back(conv_out), back(feature_grad), kernel_grad
 
 
 def solution(mesh):

time: 72.3 us -> 55.3 us (0.76)
  the two profiles are of different devices: /device:TPU:25 before, /device:TPU:0 now
where the time goes in v2:
time: 55.3 us; the launch traced here: 54.4 us
  Pallas kernels  44.4 us (80%)
  local copies, waits for them, and re-layouts  5.32 us (10%)
  other arithmetic  3.97 us (7%)
  between operations  0.64 us (1%)
    pallas_call x1, Pallas kernels, fused(): pl.pallas_call(functools.partial(body, (n, lanes)), out_shape=(jax.ShapeD...  44.4 us
    mul x1, other arithmetic, fused(): kernel_grad = jnp.transpose(kernel_grad, (1, 0, 2)).astype(f32) * scale  3.97 us
    unnamed x2, local copies, waits for them, and re-layouts  3.51 us
    transpose x1, local copies, waits for them, and re-layouts, fused(): by_frame = lambda x: jnp.transpose(x.reshape(c, frames, pixels), (1, 0, 2))  1.8 us

profile of v2, /device:TPU:0, one launch (start us, length us, event | category | flops | bytes accessed | tf_op | source)
XLA Modules:
  0.0 54.4 jit_solution(4809575468221277307)
XLA Ops:
  0.6 1.8 %copy_bitcast_fusion = (bf16[4,96,256]{2,1,0:T(8,128)(2,1)}, bf16[4,96,256]{2,1,0:T(8,128)(2,1)}) fusion(bf16[96,1,4,256]{3,2,1,0:T(4,128)(2,1)} %param.5, bf16[96,1,4,256]{3,2,1,0:T(4,128)(2,1)} %param.3), kind=kLoop, calls=%fused_computation.1 | loop fusion | bytes 786432 | tf_op jit(solution)/shard_map/transpose | solution.py:515
  2.4 44.4 %video_conv.1 = (bf16[4,96,256]{2,1,0:T(8,128)(2,1)}, bf16[4,96,256]{2,1,0:T(8,128)(2,1)}, bf16[27,96,384]{2,1,0:T(8,128)(2,1)}) custom-call(bf16[4,96,256]{2,1,0:T(8,128)(2,1)} %get-tuple-element.13.f_ref, bf16[27,96,384]{2,1,0:T(8,128)(2,1)} %bitcast.17, bf16[4,96,256]{2,1,0:T(8,128)(2,1)} %get-tuple-element.12.g_ref), custom_call_target="tpu_custom_call" | custom-call | tf_op jit(solution)/shard_map/video_conv/pallas_call | solution.py:525
  46.9 1.8 %copy.8 = bf16[96,1,4,256]{3,2,1,0:T(4,128)(2,1)} copy(bf16[96,1,4,256]{3,0,2,1:T(8,128)(2,1)} %bitcast.19) | data formatting | bytes 393216
  48.6 1.8 %copy.9 = bf16[96,1,4,256]{3,2,1,0:T(4,128)(2,1)} copy(bf16[96,1,4,256]{3,0,2,1:T(8,128)(2,1)} %bitcast.18) | data formatting | bytes 393216
  50.4 4.0 %multiply_bitcast_fusion = f32[96,27,384]{2,0,1:T(8,128)} fusion(bf16[27,96,384]{2,1,0:T(8,128)(2,1)} %get-tuple-element.8), kind=kLoop, calls=%fused_computation | loop fusion | flops 1990656 | bytes 5971968 | tf_op jit(solution)/shard_map/mul | solution.py:554

commit v3 on v2

--- a/solution.py
+++ b/solution.py
@@ -325,18 +325,28 @@
     def wait_share(held, q, sem):
         remote(held.at[q], held.at[q], right_send.at[q], sem.at[q], chan=lax.rem(z + 1, n)).wait_recv()
 
-    def relay(j):
-        @pl.when((z > 0) & (z < n - 1 - j))
+    def relay_right(j, ahead):
+        @pl.when((z > 0) & (z < n - 1 - j) & ahead)
         def _():
             wait_share(right_in, n - 1 - j, right_recv)
             add_part(right_in, n - 1 - j)
             share_right(n - 1 - j, right_in).start()
 
-        @pl.when((z < n - 1) & (z > j))
+    def relay_left(j, ahead):
+        @pl.when((z < n - 1) & (z > j) & ahead)
         def _():
             wait_share(left_in, j, left_recv)
             add_part(left_in, j)
             share_left(j, left_in).start()
+
+    def relay(j):
+        lower = 2 * z < n
+        if j < n - 1:
+            relay_right(j, lower)
+            relay_left(j, jnp.logical_not(lower))
+        if j > 0:
+            relay_right(j - 1, jnp.logical_not(lower))
+            relay_left(j - 1, lower)
 
     def ready_after(i):
         first, last = i * lanes // c, ((i + 1) * lanes - 1) // c
@@ -399,9 +409,9 @@
                 if u == 0:
                     edge_copy().wait_recv()
                 out_ref[u] = (value + edge_in[u]).astype(jnp.bfloat16)
-        if step + 1 < n - 1:
+        if step + 1 < n:
             relay(step + 1)
-    for j in range(len(later) + 1, n - 1):
+    for j in range(len(later) + 1, n):
         relay(j)
 
     def done_copy(i, a):
@@ -520,6 +530,7 @@
     half = c // 2
     lanes = 128
     pieces = 3 * (full // lanes)
+    limit = 8 * 2**20 + kernel.size * 14 + features.size * 64
     halves = pltpu.VMEM((pieces, 9, half, lanes), b16)
     shards = pltpu.VMEM((n, frames, c, pixels), b16)
     conv_out, feature_grad, kernel_grad = pl.pallas_call(
@@ -547,7 +558,7 @@
             dma((pieces,)), dma((pieces,)), dma((pieces,)), dma((pieces,)), dma((pieces,)), dma((pieces,)), dma, dma,
         ],
         compiler_params=pltpu.CompilerParams(
-            collective_id=0, has_side_effects=True, vmem_limit_bytes=56 * 2**20
+            collective_id=0, has_side_effects=True, vmem_limit_bytes=limit
         ),
         name="video_conv",
     )(by_frame(features), jnp.transpose(kernel, (1, 0, 2)), by_frame(cotangent))

time: 55.3 us -> 45 us (0.81); the launches traced: 54.4 us -> 44.8 us
  Pallas kernels: 44.4 us -> 37.5 us
  other arithmetic: 3.97 us -> 2.42 us
  local copies, waits for them, and re-layouts: 5.32 us -> 4.27 us
    pallas_call x1, Pallas kernels: 44.4 us -> 37.5 us  [fused(): pl.pallas_call(functools.partial(body, (n, lanes)), out_shape=(jax.ShapeD...]
    mul x1, other arithmetic: 3.97 us -> 2.42 us  [fused(): kernel_grad = jnp.transpose(kernel_grad, (1, 0, 2)).astype(f32) * scale]
    transpose x1, local copies, waits for them, and re-layouts: 1.8 us -> 1.06 us  [fused(): by_frame = lambda x: jnp.transpose(x.reshape(c, frames, pixels), (1, 0, 2))]
    unnamed x2 -> x4, local copies, waits for them, and re-layouts: 3.51 us -> 3.21 us
where the time goes in v3:
time: 45 us; the launch traced here: 44.8 us
  Pallas kernels  37.5 us (83%)
  local copies, waits for them, and re-layouts  4.27 us (9%)
  other arithmetic  2.42 us (5%)
  between operations  0.65 us (1%)
    pallas_call x1, Pallas kernels, fused(): pl.pallas_call(functools.partial(body, (n, lanes)), out_shape=(jax.ShapeD...  37.5 us
    unnamed x4, local copies, waits for them, and re-layouts  3.21 us
    mul x1, other arithmetic, fused(): kernel_grad = jnp.transpose(kernel_grad, (1, 0, 2)).astype(f32) * scale  2.42 us
    transpose x1, local copies, waits for them, and re-layouts, fused(): by_frame = lambda x: jnp.transpose(x.reshape(c, frames, pixels), (1, 0, 2))  1.06 us

profile of v3, /device:TPU:0, one launch (start us, length us, event | category | flops | bytes accessed | tf_op | source)
XLA Modules:
  0.0 44.8 jit_solution(17734944834785251999)
XLA Ops:
  0.6 1.1 %copy_bitcast_fusion = (bf16[4,96,256]{2,1,0:T(8,128)(2,1)S(1)}, bf16[4,96,256]{2,1,0:T(8,128)(2,1)S(1)}) fusion(bf16[96,1,4,256]{3,2,1,0:T(4,128)(2,1)} %param.5, bf16[96,1,4,256]{3,2,1,0:T(4,128)(2,1)} %param.3), kind=kLoop, calls=%fused_computation.1 | loop fusion | bytes 786432 | tf_op jit(solution)/shard_map/transpose | solution.py:525
  1.7 0.0 copy-start
  1.7 1.5 %copy-done = bf16[96,27,384]{2,0,1:T(8,128)(2,1)S(1)} copy-done((bf16[96,27,384]{2,0,1:T(8,128)(2,1)S(1)}, bf16[96,27,384]{2,0,1:T(8,128)(2,1)}, u32[]{:S(2)}) %copy-start) | copy-done | bytes 1990680
  3.3 37.5 %video_conv.1 = (bf16[4,96,256]{2,1,0:T(8,128)(2,1)S(1)}, bf16[4,96,256]{2,1,0:T(8,128)(2,1)S(1)}, bf16[27,96,384]{2,1,0:T(8,128)(2,1)S(1)}) custom-call(bf16[4,96,256]{2,1,0:T(8,128)(2,1)S(1)} %get-tuple-element.13.f_ref, bf16[27,96,384]{2,1,0:T(8,128)(2,1)S(1)} %bitcast.17, bf16[4,96,256]{2,1,0:T(8,128)(2,1)S(1)} %get-tuple-element.12.g_ref), custom_call_target="tpu_custom_call" | custom-call | tf_op jit(solution)/shard_map/video_conv/pallas_call | solution.py:536
  40.8 0.8 %copy.8 = bf16[96,1,4,256]{3,2,1,0:T(4,128)(2,1)} copy(bf16[96,1,4,256]{3,0,2,1:T(8,128)(2,1)S(1)} %bitcast.19) | data formatting | bytes 393216
  41.6 0.8 %copy.9 = bf16[96,1,4,256]{3,2,1,0:T(4,128)(2,1)} copy(bf16[96,1,4,256]{3,0,2,1:T(8,128)(2,1)S(1)} %bitcast.18) | data formatting | bytes 393216
  42.4 2.4 %multiply_bitcast_fusion = f32[96,27,384]{2,0,1:T(8,128)} fusion(bf16[27,96,384]{2,1,0:T(8,128)(2,1)S(1)} %get-tuple-element.8), kind=kLoop, calls=%fused_computation | loop fusion | flops 1990656 | bytes 5971968 | tf_op jit(solution)/shard_map/mul | solution.py:565
Async XLA Ops:
  1.7 1.6 %copy-start = (bf16[96,27,384]{2,0,1:T(8,128)(2,1)S(1)}, bf16[96,27,384]{2,0,1:T(8,128)(2,1)}, u32[]{:S(2)}) copy-start(bf16[96,27,384]{2,0,1:T(8,128)(2,1)} %param.4) | copy-start | bytes 5971972
